TPU v7x, 32 devices: a whole 2x2x4 slice. The times are simulated.
32 devices in a mesh: groups: 2 (over y), seq: 4 (over z), mp: 2 (over x), enc: 2 (over core).
Axes of the slice: x: 2, y: 2, z: 4, core: 2. Of those that a mesh axis runs over, the one named last changes fastest.
Arguments:
- tokens: bfloat16 [4096, 4096], P(('groups', 'seq'), ('mp', 'enc')), parts along dimension 0, may hold values from -6 to 6
- nbr_feats: bfloat16 [192, 128, 4096], P(('groups', 'seq'), None, ('mp', 'enc')), parts along dimension 0, may hold values from -6 to 6
- counts: int32 [8], P('groups'), parts along dimension 0, may hold values from 8 to 24, as said below
- slot_target: int32 [192], P(('groups', 'seq')), parts along dimension 0, may hold values from 0 to 63, as said below
- w_query: bfloat16 [4096, 512], P(None, ('mp', 'enc')), may hold values from -32 to 32
- w_keyval: bfloat16 [4096, 512], P(None, ('mp', 'enc')), may hold values from -1 to 1
Outputs:
- attended: bfloat16 [4096, 512], P(('groups', 'seq'), ('mp', 'enc')), parts along dimension 0
There are 2 independent parts, one for each index of `groups`. A program takes and returns all parts, laid end to end along the dimension named above; an argument that names none is the same for every part. Nothing has to cross between parts.
Inputs may be any that keep to these rules, and one draw needn't show every extreme that they name: Each seq index's live slots are its first counts slots; the counts sum to 64. `slot_target`: A live slot holds neighbour o * 16 + l of the spans of seq index o; every neighbour is held by exactly one live slot; the live slots of one seq index hold at most 8 neighbours of any one seq index; dead slots hold arbitrary values of the range.
All inputs are finite; a program needn't handle non-finite values.
Results may differ from a plain program's by a relative error of at most 0.003.
The roundings to bfloat16 on the way count: a program that leaves them out, or rounds other values in their place, can miss the bound.
Values may be sent and summed in bfloat16 or wider, within the bound.
A program may use at most 128 MiB of HBM per device.

v0:
```python
import jax
import jax.numpy as jnp
from jax import lax
from jax.sharding import PartitionSpec as P

D = 4096
SPAN = 64
NBR = 2
RLEN = 128
CH_SEQ = 8
NB_SEQ = 16
ENC_CAP = 24
epsilon = 1e-05


def partner_2(block, axis, stride):
    count = lax.axis_size(axis)
    route = []
    for low in range(count):
        high = low | 1 << stride
        if high != low and high < count:
            route += [(low, high), (high, low)]
    return lax.ppermute(block, axis, route)


def passed_along(block, axis, distance):
    devices = range(lax.axis_size(axis))
    route = [(i - distance, i) for i in devices if i - distance in devices]
    return lax.ppermute(block, axis, route)


def project_fold(weight, piece):
    width = piece.shape[-1]
    flat_rows = piece.reshape(-1, width)
    running = jnp.dot(flat_rows, weight, preferred_element_type=jnp.float32)
    widened = flat_rows.astype(jnp.float32)
    squares = jnp.sum(widened * widened, axis=1)
    return (running, squares)


def normalized(carry, factor):
    running, squares = carry
    scale_rows = lax.rsqrt(squares / D + epsilon) * factor
    return (running * scale_rows[:, None]).astype(jnp.bfloat16)


def routing_plan(slot_target, counts, pair_cap):
    seq_count = counts.shape[0]
    seq_here = lax.axis_index("seq")
    live_count = jnp.sum(jnp.where(jnp.arange(seq_count) == seq_here, counts, 0))
    slot_ids = jnp.arange(ENC_CAP)
    live_slots = slot_ids < live_count
    owner_of = slot_target // NB_SEQ
    position = slot_target % NB_SEQ
    same_owner = (
        (owner_of[:, None] == owner_of[None, :])
        & live_slots[None, :]
        & (slot_ids[None, :] < slot_ids[:, None])
    )
    rank_within = jnp.sum(same_owner.astype(jnp.int32), axis=1)
    target_slot = owner_of * pair_cap + rank_within
    buffer_ids = jnp.arange(seq_count * pair_cap)
    chosen = (buffer_ids[:, None] == target_slot[None, :]) & live_slots[None, :]
    sent_ids = jnp.sum(jnp.where(chosen, position[None, :] + 1, 0), axis=1) - 1
    return (chosen, sent_ids.reshape(seq_count, pair_cap))


def pack_rows(chosen, payload, seq_count, pair_cap):
    packed = jnp.dot(chosen.astype(jnp.bfloat16), payload, preferred_element_type=jnp.float32)
    return packed.astype(jnp.bfloat16).reshape(seq_count, pair_cap, payload.shape[1])


def place_rows(received, received_ids):
    flat_rows = received.reshape(-1, received.shape[-1])
    picker = received_ids.reshape(1, -1) == jnp.arange(NB_SEQ)[:, None]
    placed = jnp.dot(picker.astype(jnp.bfloat16), flat_rows, preferred_element_type=jnp.float32)
    return placed.astype(jnp.bfloat16)


def local(tokens, nbr_feats, counts, slot_target, w_query, w_keyval):
    seq_count = lax.axis_size("seq")
    pair_cap = max(2, 2 * NB_SEQ // seq_count)
    head_size = w_keyval.shape[1]
    chosen, sent_ids = routing_plan(slot_target, counts, pair_cap)
    folded = project_fold(w_keyval, lax.all_gather(nbr_feats, ("mp", "enc"), axis=2, tiled=True))
    encoded = normalized(folded, 1.0).reshape(ENC_CAP, RLEN * head_size)
    packed = pack_rows(chosen, encoded, seq_count, pair_cap)
    received, received_ids = (
        lax.all_to_all(packed, "seq", split_axis=0, concat_axis=0, tiled=True),
        lax.all_to_all(sent_ids, "seq", split_axis=0, concat_axis=0, tiled=True),
    )
    own_half = place_rows(received, received_ids).reshape(NB_SEQ, RLEN, head_size)
    partner = partner_2(own_half, "enc", 0)
    first_lane = lax.axis_index("enc") == 0
    key_rows = jnp.where(first_lane, own_half, partner).reshape(CH_SEQ, NBR * RLEN, head_size)
    value_rows = jnp.where(first_lane, partner, own_half).reshape(CH_SEQ, NBR * RLEN, head_size)
    prior_keys, prior_values = passed_along((key_rows[-1], value_rows[-1]), "seq", 1)
    context_keys = jnp.concatenate([prior_keys[None], key_rows[:-1]], axis=0)
    context_values = jnp.concatenate([prior_values[None], value_rows[:-1]], axis=0)
    folded_tokens = project_fold(w_query, lax.all_gather(tokens, ("mp", "enc"), axis=1, tiled=True))
    queries = normalized(folded_tokens, head_size ** (-0.5)).reshape(CH_SEQ, SPAN, head_size)
    scores = jnp.einsum("cqd,ckd->cqk", queries, context_keys, preferred_element_type=jnp.float32)
    weights = jax.nn.softmax(scores, axis=-1).astype(jnp.bfloat16)
    attended = jnp.einsum(
        "cqk,ckd->cqd", weights, context_values, preferred_element_type=jnp.float32
    )
    return attended.astype(jnp.bfloat16).reshape(CH_SEQ * SPAN, head_size)


def solution(mesh):
    placed = (
        P(("groups", "seq"), ("mp", "enc")),
        P(("groups", "seq"), None, ("mp", "enc")),
        P("groups"),
        P(("groups", "seq")),
        P(None, ("mp", "enc")),
        P(None, ("mp", "enc")),
    )
    return jax.shard_map(
        local,
        mesh=mesh,
        in_specs=placed,
        out_specs=P(("groups", "seq"), ("mp", "enc")),
        check_vma=False,
    )
```

profile of v0, /device:TPU:16, one launch (start us, length us, event | category | flops | bytes accessed | tf_op | source)
XLA Modules:
  0.0 241.7 jit_solution(9443308790571083364)
XLA Ops:
  6.5 0.7 all-gather.5.cloned.1.call-update
  7.3 0.0 all-gather.3.cloned.1.call-start
  7.3 0.7 all-gather.3.cloned.1.call-update
  8.1 0.6 fusion.24
  8.7 0.6 iota_compare_fusion.4
  9.3 0.2 convert_reduce_fusion
  9.5 0.1 select_reduce_fusion
  9.6 0.7 sub.20
  10.3 5.2 %all-to-all-start = ((s32[4,1,8]{2,1,0:T(1,128)}), s32[4,1,8]{2,1,0:T(1,128)S(1)}, u32[]{:S(2)}, u32[]{:S(2)}) async-start(s32[4,1,8]{2,1,0:T(1,128)} %bitcast.1), calls=%async_computation | async-start | bytes 4096 | tf_op jit(solution)/shard_map/all_to_all | solution.py:90
  15.5 149.4 %all-gather.5.cloned.1.call-done = bf16[24,128,4096]{2,1,0:T(8,128)(2,1)} async-done(((bf16[24,128,1024]{2,1,0:T(8,128)(2,1)}), bf16[24,128,4096]{2,1,0:T(8,128)(2,1)}) %all-gather.5.cloned.1.call-update) | async-done | bytes 25165840 | tf_op jit(solution)/shard_map/all_gather | solution.py:85
  164.9 10.6 %multiply_reduce_fusion = f32[24,128]{1,0:T(8,128)S(1)} fusion(bf16[24,128,4096]{2,1,0:T(8,128)(2,1)} %all-gather.5.cloned.1.call-done), kind=kLoop, calls=%fused_computation.1 | loop fusion | flops 37745664 | bytes 25178112 | tf_op jit(solution)/shard_map/reduce_sum | solution.py:37
  175.6 12.0 %fusion.2 = bf16[3072,128]{1,0:T(8,128)(2,1)S(1)} fusion(bf16[3072,4096]{1,0:T(8,128)(2,1)} %bitcast.30, bf16[4096,128]{1,0:T(8,128)(2,1)S(1)} %copy-done, f32[3072]{0:T(1024)S(1)} %rsqrt_bitcast_fusion), kind=kOutput, calls=%fused_computation.7 | convolution fusion | flops 3222011904 | bytes 27013120 | tf_op jit(solution)/shard_map/dot_general | solution.py:35
  187.6 0.3 reshape.81
  188.0 1.5 fusion.1
  189.5 5.1 %all-to-all-start.1 = ((bf16[4,8,16384]{2,1,0:T(8,128)(2,1)}), bf16[4,8,16384]{2,1,0:T(8,128)(2,1)S(1)}, u32[]{:S(2)}, u32[]{:S(2)}) async-start(bf16[4,8,16384]{2,1,0:T(8,128)(2,1)} %fusion.1), calls=%async_computation.1 | async-start | bytes 2097152 | tf_op jit(solution)/shard_map/all_to_all | solution.py:89
  194.6 0.5 broadcast.93
  195.1 0.7 reduce.4
  195.8 0.1 eq.61
  195.9 21.7 %all-to-all-done.1 = bf16[4,8,16384]{2,1,0:T(8,128)(2,1)S(1)} async-done(((bf16[4,8,16384]{2,1,0:T(8,128)(2,1)}), bf16[4,8,16384]{2,1,0:T(8,128)(2,1)S(1)}, u32[]{:S(2)}, u32[]{:S(2)}) %all-to-all-start.1) | async-done | bytes 1048608 | tf_op jit(solution)/shard_map/all_to_all | solution.py:89
  217.6 0.3 fusion.4
  217.8 0.1 copy.9
  217.9 0.1 collective-permute-start
  218.0 0.0 all-gather.3.cloned.1.call-done
  218.1 3.2 %multiply_reduce_fusion.1 = f32[512]{0:T(512)S(1)} fusion(bf16[512,4096]{1,0:T(8,128)(2,1)} %all-gather.3.cloned.1.call-done), kind=kLoop, calls=%fused_computation.5 | loop fusion | flops 6290944 | bytes 4196352 | tf_op jit(solution)/shard_map/reduce_sum | solution.py:37
  221.3 0.1 broadcast_select_fusion.1
  221.5 4.3 %collective-permute-start.1 = (bf16[256,128]{1,0:T(8,128)(2,1)S(1)}, bf16[256,128]{1,0:T(8,128)(2,1)S(1)}, u32[]{:S(2)}, u32[]{:S(2)}) collective-permute-start(bf16[256,128]{1,0:T(8,128)(2,1)S(1)} %bitcast.39), channel_id=1, source_target_pairs={{0,4},{4,8},{8,12},{1,5},{5,9},{9,13},{2,6},{6,10},{10,14},{3,7},{... | collective-permute-start | bytes 196616 | tf_op jit(solution)/shard_map/ppermute | solution.py:29
  225.8 1.3 fusion.6
  227.1 1.9 collective-permute-start.2
  229.1 0.3 fusion.8
  229.4 0.5 fusion.31
  229.8 3.4 %collective-permute-done.2 = bf16[256,128]{1,0:T(8,128)(2,1)S(1)} collective-permute-done((bf16[256,128]{1,0:T(8,128)(2,1)S(1)}, bf16[256,128]{1,0:T(8,128)(2,1)S(1)}, u32[]{:S(2)}, u32[]{:S(2)}) %collective-permute-start.2) | collective-permute-done | bytes 65568 | tf_op jit(solution)/shard_map/ppermute | solution.py:29
  233.3 1.6 convolution_convert_fusion.2
  (23 shorter events, 0.2 us)
Async XLA Ops:
  6.5 169.0 %copy-start = (bf16[4096,128]{1,0:T(8,128)(2,1)S(1)}, bf16[4096,128]{1,0:T(8,128)(2,1)}, u32[]{:S(2)}) copy-start(bf16[4096,128]{1,0:T(8,128)(2,1)} %param.11) | copy-start | bytes 3145732
  6.5 1.5 copy-start.3
  6.5 1.5 copy-start.4
  6.5 158.4 %all-gather.5.cloned.1.call-start = ((), (), s32[]{:S(2)}) async-start(), calls=%async_computation.3 | async-start | bytes 31457280 | tf_op jit(solution)/shard_map/all_gather | solution.py:85
  7.3 210.8 %all-gather.3.cloned.1.call-start = ((), (), s32[]{:S(2)}) async-start(), calls=%async_computation.2 | async-start | bytes 5242880 | tf_op jit(solution)/shard_map/all_gather | solution.py:100
  10.3 179.2 %all-to-all-start = ((s32[4,1,8]{2,1,0:T(1,128)}), s32[4,1,8]{2,1,0:T(1,128)S(1)}, u32[]{:S(2)}, u32[]{:S(2)}) async-start(s32[4,1,8]{2,1,0:T(1,128)} %bitcast.1), calls=%async_computation | async-start | bytes 4096 | tf_op jit(solution)/shard_map/all_to_all | solution.py:90
  189.5 28.0 %all-to-all-start.1 = ((bf16[4,8,16384]{2,1,0:T(8,128)(2,1)}), bf16[4,8,16384]{2,1,0:T(8,128)(2,1)S(1)}, u32[]{:S(2)}, u32[]{:S(2)}) async-start(bf16[4,8,16384]{2,1,0:T(8,128)(2,1)} %fusion.1), calls=%async_computation.1 | async-start | bytes 2097152 | tf_op jit(solution)/shard_map/all_to_all | solution.py:89
  217.9 3.4 %collective-permute-start = (bf16[16,128,128]{2,1,0:T(8,128)(2,1)S(1)}, bf16[16,128,128]{2,1,0:T(8,128)(2,1)S(1)}, u32[]{:S(2)}, u32[]{:S(2)}) collective-permute-start(bf16[16,128,128]{2,1,0:T(8,128)(2,1)S(1)} %bitcast.31), channel_id=1, source_target_pairs={{0,1},{1,0},{2,3},{3,2},{4,5},{5,4},{6,7},{7,6},{8,9},{9,8},{10,11... | collective-permute-start | bytes 1572872 | tf_op jit(solution)/shard_map/ppermute | solution.py:23
  218.0 7.7 %copy-start.1 = (bf16[512,4096]{1,0:T(8,128)(2,1)S(1)}, bf16[512,4096]{1,0:T(8,128)(2,1)}, u32[]{:S(2)}) copy-start(bf16[512,4096]{1,0:T(8,128)(2,1)} %all-gather.3.cloned.1.call-done) | copy-start | bytes 12582916
  218.1 7.7 %copy-start.2 = (bf16[4096,128]{1,0:T(8,128)(2,1)S(1)}, bf16[4096,128]{1,0:T(8,128)(2,1)}, u32[]{:S(2)}) copy-start(bf16[4096,128]{1,0:T(8,128)(2,1)} %param.10) | copy-start | bytes 3145732
  221.5 7.6 %collective-permute-start.1 = (bf16[256,128]{1,0:T(8,128)(2,1)S(1)}, bf16[256,128]{1,0:T(8,128)(2,1)S(1)}, u32[]{:S(2)}, u32[]{:S(2)}) collective-permute-start(bf16[256,128]{1,0:T(8,128)(2,1)S(1)} %bitcast.39), channel_id=1, source_target_pairs={{0,4},{4,8},{8,12},{1,5},{5,9},{9,13},{2,6},{6,10},{10,14},{3,7},{... | collective-permute-start | bytes 196616 | tf_op jit(solution)/shard_map/ppermute | solution.py:29
  227.1 6.2 %collective-permute-start.2 = (bf16[256,128]{1,0:T(8,128)(2,1)S(1)}, bf16[256,128]{1,0:T(8,128)(2,1)S(1)}, u32[]{:S(2)}, u32[]{:S(2)}) collective-permute-start(bf16[256,128]{1,0:T(8,128)(2,1)S(1)} %bitcast.40), channel_id=1, source_target_pairs={{0,4},{4,8},{8,12},{1,5},{5,9},{9,13},{2,6},{6,10},{10,14},{3,7},{... | collective-permute-start | bytes 196616 | tf_op jit(solution)/shard_map/ppermute | solution.py:29
Sparse Core Ops, SparseCore 0:
  8.9 155.9 all-gather.4
  166.5 34.4 all-gather.2
where the time goes:
time: 242 us
  waiting for transfers between devices  176 us (73%)
  matrix products  17.5 us (7%)
  starting transfers between devices  16.6 us (7%)
  other arithmetic  16.3 us (7%)
  between operations  13.6 us (6%)
    all_gather x1, waiting for transfers between devices, local(): lax.all_gather(nbr_feats, ('mp', 'enc'), axis=2, tiled=True)  149 us
    all_to_all x1, waiting for transfers between devices, local(): lax.all_to_all(packed, 'seq', split_axis=0, concat_axis=0, tiled=True)  21.7 us
    reduce_sum x2, other arithmetic, project_fold(): squares = jnp.sum(widened * widened, axis=1)  13.9 us
    dot_general x2, matrix products, project_fold(): running = jnp.dot(flat_rows, weight, preferred_element_type=jnp.float32)  13.3 us
    ppermute x2, starting transfers between devices, passed_along(): return lax.ppermute(block, axis, route)  6.2 us
    all_to_all x1, starting transfers between devices, local(): lax.all_to_all(sent_ids, 'seq', split_axis=0, concat_axis=0, tiled=True)  5.2 us
    all_to_all x1, starting transfers between devices, local(): lax.all_to_all(packed, 'seq', split_axis=0, concat_axis=0, tiled=True)  5.11 us
  transfers between devices with their start and end apart: 7, of which 3 were waited for; matrix products, arithmetic and copies ran while one was open for 14% of the time, Pallas kernels for 0%

commit v1 on v0

--- a/solution.py
+++ b/solution.py
@@ -11,6 +11,26 @@
 NB_SEQ = 16
 ENC_CAP = 24
 epsilon = 1e-05
+
+
+def manage_slot_by_axis(vector, d_out, join_dim):
+    even, z1 = (lax.psum(1, axis_name="seq"), lax.axis_index("seq"))
+    n_now = vector.shape[d_out] // even
+    tall = list(vector.shape)
+    tall[d_out] = n_now
+    z2 = tall[join_dim]
+    tall[join_dim] = z2 * even
+    far_arr = jnp.zeros(tall, vector.dtype)
+    for tick in [*range(even)]:
+        tile_out = lax.dynamic_slice_in_dim(vector, (z1 ^ tick) * n_now, n_now, axis=d_out)
+        if tick:
+            tile_out = lax.ppermute(
+                tile_out, axis_name="seq", perm=[(pp, pp ^ tick) for pp in range(even)]
+            )
+        far_arr = lax.dynamic_update_slice_in_dim(
+            far_arr, tile_out, (z1 ^ tick) * z2, axis=join_dim
+        )
+    return far_arr
 
 
 def partner_2(block, axis, stride):
@@ -86,7 +106,7 @@
     encoded = normalized(folded, 1.0).reshape(ENC_CAP, RLEN * head_size)
     packed = pack_rows(chosen, encoded, seq_count, pair_cap)
     received, received_ids = (
-        lax.all_to_all(packed, "seq", split_axis=0, concat_axis=0, tiled=True),
+        manage_slot_by_axis(packed, 0, 0),
         lax.all_to_all(sent_ids, "seq", split_axis=0, concat_axis=0, tiled=True),
     )
     own_half = place_rows(received, received_ids).reshape(NB_SEQ, RLEN, head_size)

time: 242 us -> 248 us (1.025)
  waiting for transfers between devices: 176 us -> 186 us
  starting transfers between devices: 16.6 us -> 12 us
    ppermute x0 -> x3, waiting for transfers between devices: none -> 22.1 us  [manage_slot_by_axis(): lax.ppermute(tile_out, axis_name='seq', perm=[(pp, pp ^ tick) for pp in r...]
    all_to_all x1 -> x0, waiting for transfers between devices: 21.7 us -> none  [local(): lax.all_to_all(packed, 'seq', split_axis=0, concat_axis=0, tiled=True)]
    all_gather x1, waiting for transfers between devices: 149 us -> 155 us  [local(): lax.all_gather(nbr_feats, ('mp', 'enc'), axis=2, tiled=True)]
    all_to_all x1 -> x0, starting transfers between devices: 5.11 us -> none  [local(): lax.all_to_all(packed, 'seq', split_axis=0, concat_axis=0, tiled=True)]
    ppermute x0 -> x3, starting transfers between devices: none -> 3.9 us  [manage_slot_by_axis(): lax.ppermute(tile_out, axis_name='seq', perm=[(pp, pp ^ tick) for pp in r...]
    all_to_all x1, waiting for transfers between devices: 0.01 us -> 3.12 us  [local(): lax.all_to_all(sent_ids, 'seq', split_axis=0, concat_axis=0, tiled=True)]
  transfers between devices with their start and end apart: 7 -> 9, of which waited for: 3 -> 6; matrix products, arithmetic and copies ran while one was open for 14% -> 13% of each run, Pallas kernels for 0% -> 0%
where the time goes in v1:
time: 248 us; the launch traced here: 246 us
  waiting for transfers between devices  186 us (75%)
  matrix products  16.5 us (7%)
  other arithmetic  16.2 us (7%)
  between operations  13.7 us (6%)
  starting transfers between devices  12 us (5%)
    all_gather x1, waiting for transfers between devices, local(): lax.all_gather(nbr_feats, ('mp', 'enc'), axis=2, tiled=True)  155 us
    ppermute x3, waiting for transfers between devices, manage_slot_by_axis(): lax.ppermute(tile_out, axis_name='seq', perm=[(pp, pp ^ tick) for pp in r...  22.1 us
    reduce_sum x2, other arithmetic, project_fold(): squares = jnp.sum(widened * widened, axis=1)  13.9 us
    dot_general x2, matrix products, project_fold(): running = jnp.dot(flat_rows, weight, preferred_element_type=jnp.float32)  13.3 us
  transfers between devices with their start and end apart: 9, of which 6 were waited for; matrix products, arithmetic and copies ran while one was open for 13% of the time, Pallas kernels for 0%

profile of v1, /device:TPU:16, one launch (start us, length us, event | category | flops | bytes accessed | tf_op | source)
XLA Modules:
  0.0 246.1 jit_solution(14546573068263089600)
XLA Ops:
  6.5 0.7 all-gather.5.cloned.1.call-update
  7.3 0.7 all-gather.3.cloned.1.call-update
  8.1 0.6 fusion.24
  8.7 0.6 iota_compare_fusion.4
  9.4 0.2 convert_reduce_fusion
  9.6 155.3 %all-gather.5.cloned.1.call-done = bf16[24,128,4096]{2,1,0:T(8,128)(2,1)} async-done(((bf16[24,128,1024]{2,1,0:T(8,128)(2,1)}), bf16[24,128,4096]{2,1,0:T(8,128)(2,1)}) %all-gather.5.cloned.1.call-update) | async-done | bytes 25165840 | tf_op jit(solution)/shard_map/all_gather | solution.py:105
  164.9 10.6 %multiply_reduce_fusion = f32[24,128]{1,0:T(8,128)S(1)} fusion(bf16[24,128,4096]{2,1,0:T(8,128)(2,1)} %all-gather.5.cloned.1.call-done), kind=kLoop, calls=%fused_computation.1 | loop fusion | flops 37745664 | bytes 25178112 | tf_op jit(solution)/shard_map/reduce_sum | solution.py:57
  175.5 12.0 %fusion.2 = bf16[3072,128]{1,0:T(8,128)(2,1)S(1)} fusion(bf16[3072,4096]{1,0:T(8,128)(2,1)} %bitcast.30, bf16[4096,128]{1,0:T(8,128)(2,1)S(1)} %copy-done, f32[3072]{0:T(1024)S(1)} %rsqrt_bitcast_fusion), kind=kOutput, calls=%fused_computation.7 | convolution fusion | flops 3222011904 | bytes 27013120 | tf_op jit(solution)/shard_map/dot_general | solution.py:55
  187.6 0.3 reshape.81
  187.9 0.6 fusion.1
  188.6 1.5 collective-permute-start
  190.2 0.1 select_reduce_fusion
  190.3 0.7 sub.20
  190.9 4.2 %all-to-all-start = ((s32[4,1,8]{2,1,0:T(1,128)}), s32[4,1,8]{2,1,0:T(1,128)S(1)}, u32[]{:S(2)}, u32[]{:S(2)}) async-start(s32[4,1,8]{2,1,0:T(1,128)} %bitcast.1), calls=%async_computation | async-start | bytes 4096 | tf_op jit(solution)/shard_map/all_to_all | solution.py:110
  195.1 3.1 %all-to-all-done = s32[4,1,8]{2,1,0:T(1,128)S(1)} async-done(((s32[4,1,8]{2,1,0:T(1,128)}), s32[4,1,8]{2,1,0:T(1,128)S(1)}, u32[]{:S(2)}, u32[]{:S(2)}) %all-to-all-start) | async-done | bytes 160 | tf_op jit(solution)/shard_map/all_to_all | solution.py:110
  198.3 0.5 broadcast.93
  198.8 0.7 reduce.4
  199.5 2.4 collective-permute-start.1
  201.9 15.7 %collective-permute-done.1 = bf16[1,8,16384]{2,1,0:T(8,128)(2,1)S(1)} collective-permute-done((bf16[1,8,16384]{2,1,0:T(8,128)(2,1)S(1)}, bf16[1,8,16384]{2,1,0:T(8,128)(2,1)S(1)}, u32[]{:S(2)}, u32[]{:S(2)}) %collective-permute-start.1) | collective-permute-done | bytes 262176 | tf_op jit(solution)/shard_map/ppermute | solution.py:27
  217.7 6.4 %collective-permute-done.2 = bf16[1,8,16384]{2,1,0:T(8,128)(2,1)S(1)} collective-permute-done((bf16[1,8,16384]{2,1,0:T(8,128)(2,1)S(1)}, bf16[1,8,16384]{2,1,0:T(8,128)(2,1)S(1)}, u32[]{:S(2)}, u32[]{:S(2)}) %collective-permute-start.2) | collective-permute-done | bytes 262176 | tf_op jit(solution)/shard_map/ppermute | solution.py:27
  224.1 0.3 fusion.4
  224.4 0.1 copy.9
  224.6 3.2 %multiply_reduce_fusion.1 = f32[512]{0:T(512)S(1)} fusion(bf16[512,4096]{1,0:T(8,128)(2,1)} %all-gather.3.cloned.1.call-done), kind=kLoop, calls=%fused_computation.5 | loop fusion | flops 6290944 | bytes 4196352 | tf_op jit(solution)/shard_map/reduce_sum | solution.py:57
  227.8 0.1 broadcast_select_fusion.1
  228.0 1.9 collective-permute-start.4
  229.9 1.3 fusion.6
  231.3 1.9 collective-permute-start.5
  233.2 1.1 collective-permute-done.4
  234.3 0.3 fusion.8
  234.6 0.5 fusion.31
  235.1 2.5 %collective-permute-done.5 = bf16[256,128]{1,0:T(8,128)(2,1)S(1)} collective-permute-done((bf16[256,128]{1,0:T(8,128)(2,1)S(1)}, bf16[256,128]{1,0:T(8,128)(2,1)S(1)}, u32[]{:S(2)}, u32[]{:S(2)}) %collective-permute-start.5) | collective-permute-done | bytes 65568 | tf_op jit(solution)/shard_map/ppermute | solution.py:49
  237.6 1.6 convolution_convert_fusion.2
  (32 shorter events, 0.6 us)
Async XLA Ops:
  6.5 169.0 %copy-start = (bf16[4096,128]{1,0:T(8,128)(2,1)S(1)}, bf16[4096,128]{1,0:T(8,128)(2,1)}, u32[]{:S(2)}) copy-start(bf16[4096,128]{1,0:T(8,128)(2,1)} %param.11) | copy-start | bytes 3145732
  6.5 1.5 copy-start.3
  6.5 1.5 copy-start.4
  6.5 158.3 %all-gather.5.cloned.1.call-start = ((), (), s32[]{:S(2)}) async-start(), calls=%async_computation.2 | async-start | bytes 31457280 | tf_op jit(solution)/shard_map/all_gather | solution.py:105
  7.3 217.3 %all-gather.3.cloned.1.call-start = ((), (), s32[]{:S(2)}) async-start(), calls=%async_computation.1 | async-start | bytes 5242880 | tf_op jit(solution)/shard_map/all_gather | solution.py:120
  188.6 13.2 %collective-permute-start = (bf16[1,8,16384]{2,1,0:T(8,128)(2,1)S(1)}, bf16[1,8,16384]{2,1,0:T(8,128)(2,1)S(1)}, u32[]{:S(2)}, u32[]{:S(2)}) collective-permute-start(bf16[1,8,16384]{2,1,0:T(8,128)(2,1)S(1)} %get-tuple-element.9), channel_id=1, source_target_pairs={{0,4},{4,0},{8,12},{12,8},{1,5},{5,1},{9,13},{13,9},{2,6},{6,2},{1... | collective-permute-start | bytes 786440 | tf_op jit(solution)/shard_map/ppermute | solution.py:27
  190.9 7.3 %all-to-all-start = ((s32[4,1,8]{2,1,0:T(1,128)}), s32[4,1,8]{2,1,0:T(1,128)S(1)}, u32[]{:S(2)}, u32[]{:S(2)}) async-start(s32[4,1,8]{2,1,0:T(1,128)} %bitcast.1), calls=%async_computation | async-start | bytes 4096 | tf_op jit(solution)/shard_map/all_to_all | solution.py:110
  199.5 18.1 %collective-permute-start.1 = (bf16[1,8,16384]{2,1,0:T(8,128)(2,1)S(1)}, bf16[1,8,16384]{2,1,0:T(8,128)(2,1)S(1)}, u32[]{:S(2)}, u32[]{:S(2)}) collective-permute-start(bf16[1,8,16384]{2,1,0:T(8,128)(2,1)S(1)} %get-tuple-element.8), channel_id=1, source_target_pairs={{0,8},{4,12},{8,0},{12,4},{1,9},{5,13},{9,1},{13,5},{2,10},{6,14},... | collective-permute-start | bytes 786440 | tf_op jit(solution)/shard_map/ppermute | solution.py:27
  201.9 22.2 %collective-permute-start.2 = (bf16[1,8,16384]{2,1,0:T(8,128)(2,1)S(1)}, bf16[1,8,16384]{2,1,0:T(8,128)(2,1)S(1)}, u32[]{:S(2)}, u32[]{:S(2)}) collective-permute-start(bf16[1,8,16384]{2,1,0:T(8,128)(2,1)S(1)} %get-tuple-element.7), channel_id=1, source_target_pairs={{0,12},{4,8},{8,4},{12,0},{1,13},{5,9},{9,5},{13,1},{2,14},{6,10},... | collective-permute-start | bytes 786440 | tf_op jit(solution)/shard_map/ppermute | solution.py:27
  224.5 3.4 %collective-permute-start.3 = (bf16[16,128,128]{2,1,0:T(8,128)(2,1)S(1)}, bf16[16,128,128]{2,1,0:T(8,128)(2,1)S(1)}, u32[]{:S(2)}, u32[]{:S(2)}) collective-permute-start(bf16[16,128,128]{2,1,0:T(8,128)(2,1)S(1)} %bitcast.31), channel_id=1, source_target_pairs={{0,1},{1,0},{2,3},{3,2},{4,5},{5,4},{6,7},{7,6},{8,9},{9,8},{10,11... | collective-permute-start | bytes 1572872 | tf_op jit(solution)/shard_map/ppermute | solution.py:43
  224.6 5.3 %copy-start.1 = (bf16[512,4096]{1,0:T(8,128)(2,1)S(1)}, bf16[512,4096]{1,0:T(8,128)(2,1)}, u32[]{:S(2)}) copy-start(bf16[512,4096]{1,0:T(8,128)(2,1)} %all-gather.3.cloned.1.call-done) | copy-start | bytes 12582916
  224.6 5.3 %copy-start.2 = (bf16[4096,128]{1,0:T(8,128)(2,1)S(1)}, bf16[4096,128]{1,0:T(8,128)(2,1)}, u32[]{:S(2)}) copy-start(bf16[4096,128]{1,0:T(8,128)(2,1)} %param.10) | copy-start | bytes 3145732
  228.0 6.3 %collective-permute-start.4 = (bf16[256,128]{1,0:T(8,128)(2,1)S(1)}, bf16[256,128]{1,0:T(8,128)(2,1)S(1)}, u32[]{:S(2)}, u32[]{:S(2)}) collective-permute-start(bf16[256,128]{1,0:T(8,128)(2,1)S(1)} %bitcast.39), channel_id=1, source_target_pairs={{0,4},{4,8},{8,12},{1,5},{5,9},{9,13},{2,6},{6,10},{10,14},{3,7},{... | collective-permute-start | bytes 196616 | tf_op jit(solution)/shard_map/ppermute | solution.py:49
  231.3 6.3 %collective-permute-start.5 = (bf16[256,128]{1,0:T(8,128)(2,1)S(1)}, bf16[256,128]{1,0:T(8,128)(2,1)S(1)}, u32[]{:S(2)}, u32[]{:S(2)}) collective-permute-start(bf16[256,128]{1,0:T(8,128)(2,1)S(1)} %bitcast.40), channel_id=1, source_target_pairs={{0,4},{4,8},{8,12},{1,5},{5,9},{9,13},{2,6},{6,10},{10,14},{3,7},{... | collective-permute-start | bytes 196616 | tf_op jit(solution)/shard_map/ppermute | solution.py:49
Sparse Core Ops, SparseCore 0:
  8.9 155.8 all-gather.4
  166.4 34.4 all-gather.2
